TPU v7x, 32 devices: a whole 2x2x4 slice. The times are simulated.
32 devices in a mesh: dp: 8 (over z, x), rep: 4 (over y, core).
Axes of the slice: x: 2, y: 2, z: 4, core: 2. Of those that a mesh axis runs over, the one named last changes fastest.
Arguments:
- tokens: bfloat16 [128, 256, 512], P(('dp', 'rep')), may hold values from -6 to 6
- cotangent: bfloat16 [128, 256, 512], P(('dp', 'rep')), may hold values from -6 to 6
- target_lengths: int32 [128], P(('dp', 'rep')), may hold values from 32 to 256, as said below
- task_mask: int32 [128, 256], P(('dp', 'rep')), may hold values 0 or 1
- memory_lengths: int32 [128], P(('dp', 'rep')), may hold values from 256 to 1024, as said below
- position_buckets: int32 [256, 256], replicated, may hold values from 0 to 510
- memory: bfloat16 [8, 16, 1024, 512], P(None, 'rep', 'dp'), may hold values from -6 to 6
- self_gain: float32 [512], replicated, may hold values from 0.25 to 1.75
- self_shift: float32 [512], replicated, may hold values from -1.75 to 1.75
- query_weight: bfloat16 [512, 512], replicated, may hold values from -0.25 to 0.25
- query_bias: float32 [512], replicated, may hold values from -1.75 to 1.75
- key_weight: bfloat16 [512, 512], replicated, may hold values from -0.25 to 0.25
- value_weight: bfloat16 [512, 512], replicated, may hold values from -0.25 to 0.25
- value_bias: float32 [512], replicated, may hold values from -1.75 to 1.75
- position_table: float32 [511, 8], replicated, may hold values from -6 to 6
- head_scale: float32 [8], replicated, may hold values from 0.5 to 1.5
- output_weight: bfloat16 [512, 512], replicated, may hold values from -1 to 1
- output_bias: float32 [512], replicated, may hold values from -1.75 to 1.75
- cross_gain: float32 [512], replicated, may hold values from 0.25 to 1.75
- cross_shift: float32 [512], replicated, may hold values from -1.75 to 1.75
- cross_query: bfloat16 [512, 512], replicated, may hold values from -0.25 to 0.25
- cross_query_bias: float32 [512], replicated, may hold values from -1.75 to 1.75
- cross_key: bfloat16 [512, 512], replicated, may hold values from -0.25 to 0.25
- cross_value: bfloat16 [512, 512], replicated, may hold values from -0.25 to 0.25
- cross_value_bias: float32 [512], replicated, may hold values from -1.75 to 1.75
- post_gain: float32 [512], replicated, may hold values from 0.25 to 1.75
- post_shift: float32 [512], replicated, may hold values from -1.75 to 1.75
- cross_output: bfloat16 [512, 512], replicated, may hold values from -0.25 to 0.25
- cross_output_bias: float32 [512], replicated, may hold values from -1.75 to 1.75
- feed_gain: float32 [512], replicated, may hold values from 0.25 to 1.75
- feed_shift: float32 [512], replicated, may hold values from -1.75 to 1.75
- inner_weight: bfloat16 [512, 2048], replicated, may hold values from -0.25 to 0.25
- inner_bias: float32 [2048], replicated, may hold values from -1.75 to 1.75
- inner_gain: float32 [2048], replicated, may hold values from 0.25 to 1.75
- inner_shift: float32 [2048], replicated, may hold values from -1.75 to 1.75
- outer_weight: bfloat16 [2048, 512], replicated, may hold values from -0.125 to 0.125
- outer_bias: float32 [512], replicated, may hold values from -1.75 to 1.75
Outputs:
- layer_output: bfloat16 [128, 256, 512], P(('dp', 'rep'))
- tokens_gradient: bfloat16 [128, 256, 512], P(('dp', 'rep'))
- memory_gradient: bfloat16 [8, 16, 1024, 512], P(None, 'rep', 'dp')
- gradient_self_gain: float32 [512], replicated
- gradient_self_shift: float32 [512], replicated
- gradient_query_weight: float32 [512, 512], replicated
- gradient_query_bias: float32 [512], replicated
- gradient_key_weight: float32 [512, 512], replicated
- gradient_value_weight: float32 [512, 512], replicated
- gradient_value_bias: float32 [512], replicated
- gradient_position_table: float32 [511, 8], replicated
- gradient_head_scale: float32 [8], replicated
- gradient_output_weight: float32 [512, 512], replicated
- gradient_output_bias: float32 [512], replicated
- gradient_cross_gain: float32 [512], replicated
- gradient_cross_shift: float32 [512], replicated
- gradient_cross_query: float32 [512, 512], replicated
- gradient_cross_query_bias: float32 [512], replicated
- gradient_cross_key: float32 [512, 512], replicated
- gradient_cross_value: float32 [512, 512], replicated
- gradient_cross_value_bias: float32 [512], replicated
- gradient_post_gain: float32 [512], replicated
- gradient_post_shift: float32 [512], replicated
- gradient_cross_output: float32 [512, 512], replicated
- gradient_cross_output_bias: float32 [512], replicated
- gradient_feed_gain: float32 [512], replicated
- gradient_feed_shift: float32 [512], replicated
- gradient_inner_weight: float32 [512, 2048], replicated
- gradient_inner_bias: float32 [2048], replicated
- gradient_inner_gain: float32 [2048], replicated
- gradient_inner_shift: float32 [2048], replicated
- gradient_outer_weight: float32 [2048, 512], replicated
- gradient_outer_bias: float32 [512], replicated
Inputs may be any that keep to these rules, and one draw needn't show every extreme that they name: `target_lengths`: some sequence has 256 real tokens in every draw; later positions are padding. `memory_lengths`: some sequence has all 1024 memory positions real in every draw.
All inputs are finite; a program needn't handle non-finite values. No bound on the sum of `task_mask` on one device may be relied on, other than what follows from the above.
Results may differ from a plain program's by a relative error of at most 0.017.
Values may be sent and summed in bfloat16 or wider, within the bound.
A program may use at most 192 MiB of HBM per device.

v0:
```python
import jax
import jax.numpy as jnp
from jax import lax
from jax.sharding import PartitionSpec as P

big_negative = -1e30


def layer_norm(value_in, norm_gain, norm_shift):
    center = value_in - jnp.mean(value_in, axis=-1, keepdims=True)
    spread = jnp.mean(center * center, axis=-1, keepdims=True)
    return center * lax.rsqrt(spread + 1e-05) * norm_gain + norm_shift


def gelu_exact(value_in):
    return jax.nn.gelu(value_in, approximate=False)


def matmul(left_side, right_side):
    return jnp.dot(left_side, right_side, preferred_element_type=jnp.float32)


def outer_sum(left_side, right_side):
    return lax.dot_general(
        left_side, right_side, (((0,), (0,)), ((), ())), preferred_element_type=jnp.float32
    )


def back_product(grad_in, weight):
    return lax.dot_general(
        grad_in, weight, (((grad_in.ndim - 1,), (1,)), ((), ())), preferred_element_type=jnp.float32
    )


def split_heads(matrix, head_count, seq_count, span):
    return matrix.reshape(seq_count, span, head_count, -1).transpose(2, 0, 1, 3)


def merge_heads(stacked):
    head_count, seq_count, span, head_size = stacked.shape
    return stacked.transpose(1, 2, 0, 3).reshape(seq_count * span, head_count * head_size)


def bucket_blocks(position_buckets):
    length = position_buckets.shape[0]
    row_block = 64
    return position_buckets.reshape(length // row_block, row_block, length)


def scores_of(query_block, key_block, extra_bias, allowed):
    raw_scores = (
        jnp.einsum("sqd,skd->sqk", query_block, key_block, preferred_element_type=jnp.float32)
        + extra_bias
    )
    return jnp.where(allowed, raw_scores, big_negative)


def attend_forward(query_block, key_block, value_block, extra_bias, allowed):
    scores = scores_of(query_block, key_block, extra_bias, allowed)
    row_top = jnp.max(scores, axis=-1, keepdims=True)
    weights = jnp.exp(scores - row_top)
    row_total = jnp.sum(weights, axis=-1, keepdims=True)
    rounded = (weights / row_total).astype(jnp.bfloat16)
    attended = jnp.einsum("sqk,skd->sqd", rounded, value_block, preferred_element_type=jnp.float32)
    return (attended, (row_top + jnp.log(row_total))[..., 0])


def attend_backward(query_block, key_block, value_block, extra_bias, allowed, logsum, upstream):
    scores = scores_of(query_block, key_block, extra_bias, allowed)
    weights = jnp.exp(scores - logsum[..., None])
    grad_weights = jnp.einsum(
        "sqd,skd->sqk", upstream, value_block, preferred_element_type=jnp.float32
    )
    row_inner = jnp.sum(weights * grad_weights, axis=-1, keepdims=True)
    dscores = (weights * (grad_weights - row_inner)).astype(jnp.bfloat16)
    dquery = jnp.einsum("sqk,skd->sqd", dscores, key_block, preferred_element_type=jnp.float32)
    grad_keys = jnp.einsum("sqk,sqd->skd", dscores, query_block, preferred_element_type=jnp.float32)
    dvalues = jnp.einsum(
        "sqk,sqd->skd", weights.astype(jnp.bfloat16), upstream, preferred_element_type=jnp.float32
    )
    return (dquery, grad_keys, dvalues, jnp.sum(dscores.astype(jnp.float32), axis=0))


def local(
    tokens,
    cotangent,
    target_lengths,
    task_mask,
    memory_lengths,
    position_buckets,
    memory,
    self_gain,
    self_shift,
    query_weight,
    query_bias,
    key_weight,
    value_weight,
    value_bias,
    position_table,
    head_scale,
    output_weight,
    output_bias,
    cross_gain,
    cross_shift,
    cross_query,
    cross_query_bias,
    cross_key,
    cross_value,
    cross_value_bias,
    post_gain,
    post_shift,
    cross_output,
    cross_output_bias,
    feed_gain,
    feed_shift,
    inner_weight,
    inner_bias,
    inner_gain,
    inner_shift,
    outer_weight,
    outer_bias,
):
    seq_count = tokens.shape[0]
    length = tokens.shape[1]
    model_width = tokens.shape[2]
    head_count = head_scale.shape[0]
    bucket_count = position_table.shape[0]
    row_count = seq_count * length
    mem_total = memory.shape[2] * lax.axis_size("dp")
    bucket_ids = jnp.arange(bucket_count, dtype=jnp.int32)
    bucket_rows = bucket_blocks(position_buckets)
    local_key = matmul(memory, cross_key).astype(jnp.bfloat16)
    local_value = (matmul(memory, cross_value) + cross_value_bias).astype(jnp.bfloat16)
    key_arrived, value_arrived = (
        lax.all_to_all(local_key, "dp", split_axis=0, concat_axis=2, tiled=True),
        lax.all_to_all(local_value, "dp", split_axis=0, concat_axis=2, tiled=True),
    )
    key_two = key_arrived.reshape(seq_count * mem_total, model_width)
    value_two = value_arrived.reshape(seq_count * mem_total, model_width)
    places = jnp.arange(length)
    causal = places[None, :, None] >= places[None, None, :]
    self_allowed = causal & (places[None, None, :] < target_lengths[:, None, None])
    cross_allowed = jnp.arange(mem_total)[None, None, :] < memory_lengths[:, None, None]
    stream_zero = tokens.astype(jnp.float32).reshape(row_count, model_width)
    normed_one, norm_one_back = jax.vjp(layer_norm, stream_zero, self_gain, self_shift)
    normed_one_low = normed_one.astype(jnp.bfloat16)
    query_one = ((matmul(normed_one_low, query_weight) + query_bias) * 0.125).astype(jnp.bfloat16)
    key_one = matmul(normed_one_low, key_weight).astype(jnp.bfloat16)
    value_one = (matmul(normed_one_low, value_weight) + value_bias).astype(jnp.bfloat16)

    def bias_rows(rows_ids):
        one_hot = (rows_ids[:, :, None] == bucket_ids[None, None, :]).astype(jnp.float32)
        return jnp.einsum("qkb,bh->hqk", one_hot, position_table, precision=lax.Precision.HIGHEST)

    bias_heads = jnp.transpose(lax.map(bias_rows, bucket_rows), (1, 0, 2, 3)).reshape(
        head_count, length, length
    )
    heads_query = split_heads(query_one, head_count, seq_count, length)
    heads_key = split_heads(key_one, head_count, seq_count, length)
    heads_value = split_heads(value_one, head_count, seq_count, length)

    def self_forward(packed):
        return attend_forward(packed[0], packed[1], packed[2], packed[3], self_allowed)

    out_one, logsum_one = lax.map(self_forward, (heads_query, heads_key, heads_value, bias_heads))
    mixed_one = merge_heads(out_one * head_scale[:, None, None, None]).astype(jnp.bfloat16)
    stream_one = stream_zero + matmul(mixed_one, output_weight) + output_bias
    normed_two, norm_two_back = jax.vjp(layer_norm, stream_one, cross_gain, cross_shift)
    normed_two_low = normed_two.astype(jnp.bfloat16)
    query_two = ((matmul(normed_two_low, cross_query) + cross_query_bias) * 0.125).astype(
        jnp.bfloat16
    )
    heads_query_two = split_heads(query_two, head_count, seq_count, length)
    heads_key_two = split_heads(key_two, head_count, seq_count, mem_total)
    heads_value_two = split_heads(value_two, head_count, seq_count, mem_total)

    def cross_forward(packed):
        return attend_forward(packed[0], packed[1], packed[2], 0.0, cross_allowed)

    out_two, logsum_two = lax.map(cross_forward, (heads_query_two, heads_key_two, heads_value_two))
    post_two, post_back = jax.vjp(layer_norm, merge_heads(out_two), post_gain, post_shift)
    post_low = post_two.astype(jnp.bfloat16)
    stream_two = stream_one + matmul(post_low, cross_output) + cross_output_bias
    normed_three, norm_three_back = jax.vjp(layer_norm, stream_two, feed_gain, feed_shift)
    normed_three_low = normed_three.astype(jnp.bfloat16)
    inner_pre = matmul(normed_three_low, inner_weight) + inner_bias
    activated, gelu_back = jax.vjp(gelu_exact, inner_pre)
    normed_inner, inner_back = jax.vjp(layer_norm, activated, inner_gain, inner_shift)
    normed_inner_low = normed_inner.astype(jnp.bfloat16)
    stream_three = stream_two + matmul(normed_inner_low, outer_weight) + outer_bias
    layer_output = stream_three.astype(jnp.bfloat16).reshape(seq_count, length, model_width)
    keep = task_mask.astype(jnp.float32) * (places[None, :] < target_lengths[:, None]).astype(
        jnp.float32
    )
    grad_three = (cotangent.astype(jnp.float32) * keep[:, :, None]).reshape(row_count, model_width)
    sum_outer_bias = jnp.sum(grad_three, axis=0)
    low_three = grad_three.astype(jnp.bfloat16)
    sum_outer_weight = outer_sum(normed_inner_low, low_three)
    grad_activated, sum_inner_gain, sum_inner_shift = inner_back(
        back_product(low_three, outer_weight)
    )
    grad_inner = gelu_back(grad_activated)[0]
    sum_inner_bias = jnp.sum(grad_inner, axis=0)
    low_inner = grad_inner.astype(jnp.bfloat16)
    sum_inner_weight = outer_sum(normed_three_low, low_inner)
    part_two, sum_feed_gain, sum_feed_shift = norm_three_back(back_product(low_inner, inner_weight))
    grad_two = grad_three + part_two
    sum_cross_output_bias = jnp.sum(grad_two, axis=0)
    low_two = grad_two.astype(jnp.bfloat16)
    sum_cross_output = outer_sum(post_low, low_two)
    grad_merged, sum_post_gain, sum_post_shift = post_back(back_product(low_two, cross_output))
    upstream_two = split_heads(grad_merged.astype(jnp.bfloat16), head_count, seq_count, length)

    def cross_backward(packed):
        return attend_backward(
            packed[0], packed[1], packed[2], 0.0, cross_allowed, packed[3], packed[4]
        )

    dquery_two, dkey_two, dvalue_two, unused_bias = lax.map(
        cross_backward, (heads_query_two, heads_key_two, heads_value_two, logsum_two, upstream_two)
    )
    low_query_two = merge_heads(dquery_two).astype(jnp.bfloat16) * 0.125
    low_key_two = merge_heads(dkey_two).astype(jnp.bfloat16)
    low_value_two = merge_heads(dvalue_two).astype(jnp.bfloat16)
    sum_cross_query = outer_sum(normed_two_low, low_query_two)
    sum_cross_query_bias = jnp.sum(low_query_two.astype(jnp.float32), axis=0)
    sum_cross_value_bias = jnp.sum(low_value_two.astype(jnp.float32), axis=0)
    key_back, value_back = (
        lax.all_to_all(
            low_key_two.reshape(1, seq_count, mem_total, model_width),
            "dp",
            split_axis=2,
            concat_axis=0,
            tiled=True,
        ),
        lax.all_to_all(
            low_value_two.reshape(1, seq_count, mem_total, model_width),
            "dp",
            split_axis=2,
            concat_axis=0,
            tiled=True,
        ),
    )
    memory_gradient = (
        back_product(key_back, cross_key) + back_product(value_back, cross_value)
    ).astype(jnp.bfloat16)
    sum_cross_key = lax.dot_general(
        memory, key_back, (((0, 1, 2), (0, 1, 2)), ((), ())), preferred_element_type=jnp.float32
    )
    sum_cross_value = lax.dot_general(
        memory, value_back, (((0, 1, 2), (0, 1, 2)), ((), ())), preferred_element_type=jnp.float32
    )
    part_one, sum_cross_gain, sum_cross_shift = norm_two_back(
        back_product(low_query_two, cross_query)
    )
    grad_one = grad_two + part_one
    sum_output_bias = jnp.sum(grad_one, axis=0)
    low_one = grad_one.astype(jnp.bfloat16)
    sum_output_weight = outer_sum(mixed_one, low_one)
    grad_mixed = split_heads(back_product(low_one, output_weight), head_count, seq_count, length)
    sum_head_scale = jnp.sum(out_one * grad_mixed, axis=(1, 2, 3))
    upstream_one = (grad_mixed * head_scale[:, None, None, None]).astype(jnp.bfloat16)

    def self_backward(packed):
        return attend_backward(
            packed[0], packed[1], packed[2], packed[3], self_allowed, packed[4], packed[5]
        )

    dquery_one, dkey_one, dvalue_one, bias_grads = lax.map(
        self_backward, (heads_query, heads_key, heads_value, bias_heads, logsum_one, upstream_one)
    )
    block_count = bucket_rows.shape[0]
    grad_blocks = jnp.transpose(
        bias_grads.reshape(head_count, block_count, length // block_count, length), (1, 0, 2, 3)
    )

    def bucket_sums(total, packed):
        one_hot = (packed[0][:, :, None] == bucket_ids[None, None, :]).astype(jnp.float32)
        return (
            total + jnp.einsum("qkb,hqk->bh", one_hot, packed[1], precision=lax.Precision.HIGHEST),
            None,
        )

    sum_position_table, unused_end = lax.scan(
        bucket_sums, jnp.zeros((bucket_count, head_count), jnp.float32), (bucket_rows, grad_blocks)
    )
    low_query_one = merge_heads(dquery_one).astype(jnp.bfloat16) * 0.125
    low_key_one = merge_heads(dkey_one).astype(jnp.bfloat16)
    low_value_one = merge_heads(dvalue_one).astype(jnp.bfloat16)
    sum_query_weight = outer_sum(normed_one_low, low_query_one)
    sum_query_bias = jnp.sum(low_query_one.astype(jnp.float32), axis=0)
    sum_key_weight = outer_sum(normed_one_low, low_key_one)
    sum_value_weight = outer_sum(normed_one_low, low_value_one)
    sum_value_bias = jnp.sum(low_value_one.astype(jnp.float32), axis=0)
    grad_normed_one = (
        back_product(low_query_one, query_weight)
        + back_product(low_key_one, key_weight)
        + back_product(low_value_one, value_weight)
    )
    part_zero, sum_self_gain, sum_self_shift = norm_one_back(grad_normed_one)
    tokens_gradient = (
        (grad_one + part_zero).astype(jnp.bfloat16).reshape(seq_count, length, model_width)
    )
    totals = lax.psum(
        (
            sum_self_gain,
            sum_self_shift,
            sum_query_weight,
            sum_query_bias,
            sum_key_weight,
            sum_value_weight,
            sum_value_bias,
            sum_position_table,
            sum_head_scale,
            sum_output_weight,
            sum_output_bias,
            sum_cross_gain,
            sum_cross_shift,
            sum_cross_query,
            sum_cross_query_bias,
            sum_cross_key,
            sum_cross_value,
            sum_cross_value_bias,
            sum_post_gain,
            sum_post_shift,
            sum_cross_output,
            sum_cross_output_bias,
            sum_feed_gain,
            sum_feed_shift,
            sum_inner_weight,
            sum_inner_bias,
            sum_inner_gain,
            sum_inner_shift,
            sum_outer_weight,
            sum_outer_bias,
        ),
        ("dp", "rep"),
    )
    return (layer_output, tokens_gradient, memory_gradient) + tuple(totals)


def solution(mesh):
    in_specs = (
        P(("dp", "rep"), None, None),
        P(("dp", "rep"), None, None),
        P(("dp", "rep")),
        P(("dp", "rep"), None),
        P(("dp", "rep")),
        P(),
        P(None, "rep", "dp", None),
        P(),
        P(),
        P(),
        P(),
        P(),
        P(),
        P(),
        P(),
        P(),
        P(),
        P(),
        P(),
        P(),
        P(),
        P(),
        P(),
        P(),
        P(),
        P(),
        P(),
        P(),
        P(),
        P(),
        P(),
        P(),
        P(),
        P(),
        P(),
        P(),
        P(),
    )
    out_specs = (
        P(("dp", "rep"), None, None),
        P(("dp", "rep"), None, None),
        P(None, "rep", "dp", None),
        P(),
        P(),
        P(),
        P(),
        P(),
        P(),
        P(),
        P(),
        P(),
        P(),
        P(),
        P(),
        P(),
        P(),
        P(),
        P(),
        P(),
        P(),
        P(),
        P(),
        P(),
        P(),
        P(),
        P(),
        P(),
        P(),
        P(),
        P(),
        P(),
        P(),
    )
    return jax.shard_map(local, mesh=mesh, in_specs=in_specs, out_specs=out_specs, check_vma=False)
```

profile of v0, /device:TPU:10, one launch (start us, length us, event | category | flops | bytes accessed | tf_op | source)
XLA Modules:
  0.0 1247.0 jit_solution(17681116033645077815)
XLA Ops:
  7.2 6.8 convolution_convert_fusion
  14.0 6.3 all-to-all-start
  51.6 77.0 %while.86 = (s32[]{:T(128)}, f32[4,8,64,256]{3,1,2,0:T(8,128)}, s32[4,64,256]{2,1,0:T(8,128)}, f32[511,8]{0,1:T(8,128)S(1)}) while((s32[]{:T(128)}, f32[4,8,64,256]{3,1,2,0:T(8,128)}, s32[4,64,256]{2,1,0:T(8,128)}, f32[511,8]{0,1:T(8,128)S(1)}) %tuple.235), condition=%wide.region_3.4_spmd.clone.clone, body=%wide.region_2.3_spmd.clone.sunk.clone | while | flops 812105728 | bytes 737817 | solution.py:155
  52.5 18.4 %fusion.310 = f32[4,8,64,256]{3,1,2,0:T(8,128)} fusion(f32[4,8,64,256]{3,1,2,0:T(8,128)} %get-tuple-element.1226, s32[]{:T(128)} %get-tuple-element.1225, s32[64,256]{1,0:T(8,128)S(1)} %dynamic-slice_bitcast_fusion.18, f32[511,8]{0,1:T(8,128)S(1)} %get-tuple-element.1232), kind=kOutput, calls=%fused_computation.10.clone.1.clone | convolution fusion | flops 812105728 | bytes 606688 | tf_op jit(solution)/shard_map/while/body/eval_jaxpr/qkb,bh->hqk/dot_general | solution.py:153
  71.7 18.4 %fusion.310 = f32[4,8,64,256]{3,1,2,0:T(8,128)} fusion(f32[4,8,64,256]{3,1,2,0:T(8,128)} %get-tuple-element.1226, s32[]{:T(128)} %get-tuple-element.1225, s32[64,256]{1,0:T(8,128)S(1)} %dynamic-slice_bitcast_fusion.18, f32[511,8]{0,1:T(8,128)S(1)} %get-tuple-element.1232), kind=kOutput, calls=%fused_computation.10.clone.1.clone | convolution fusion | flops 812105728 | bytes 606688 | tf_op jit(solution)/shard_map/while/body/eval_jaxpr/qkb,bh->hqk/dot_general | solution.py:153
  91.0 18.4 %fusion.310 = f32[4,8,64,256]{3,1,2,0:T(8,128)} fusion(f32[4,8,64,256]{3,1,2,0:T(8,128)} %get-tuple-element.1226, s32[]{:T(128)} %get-tuple-element.1225, s32[64,256]{1,0:T(8,128)S(1)} %dynamic-slice_bitcast_fusion.18, f32[511,8]{0,1:T(8,128)S(1)} %get-tuple-element.1232), kind=kOutput, calls=%fused_computation.10.clone.1.clone | convolution fusion | flops 812105728 | bytes 606688 | tf_op jit(solution)/shard_map/while/body/eval_jaxpr/qkb,bh->hqk/dot_general | solution.py:153
  110.2 18.4 %fusion.310 = f32[4,8,64,256]{3,1,2,0:T(8,128)} fusion(f32[4,8,64,256]{3,1,2,0:T(8,128)} %get-tuple-element.1226, s32[]{:T(128)} %get-tuple-element.1225, s32[64,256]{1,0:T(8,128)S(1)} %dynamic-slice_bitcast_fusion.18, f32[511,8]{0,1:T(8,128)S(1)} %get-tuple-element.1232), kind=kOutput, calls=%fused_computation.10.clone.1.clone | convolution fusion | flops 812105728 | bytes 606688 | tf_op jit(solution)/shard_map/while/body/eval_jaxpr/qkb,bh->hqk/dot_general | solution.py:153
  131.7 6.7 add_convert_fusion.2
  138.3 6.3 all-to-all-start.1
  144.6 37.2 %while.87 = (s32[]{:T(128)}, f32[8,4,256,64]{2,1,3,0:T(4,128)}, f32[8,4,256]{2,1,0:T(4,128)S(1)}, bf16[8,4,256,64]{2,3,1,0:T(8,128)(2,1)}, bf16[8,4,256,64]{2,3,...) while((s32[]{:T(128)}, f32[8,4,256,64]{2,1,3,0:T(4,128)}, ...), condition=%wide.region_7.8_spmd.clone.clone, body=%wide.region_4.7_spmd.clone.sunk.clone | while | flops 69467136 | bytes 5213285 | solution.py:165
  201.2 7.6 copy.149
  208.7 7.3 reshape_reshape.6
  216.0 4.9 copy.152
  220.9 12.9 %all-to-all-done.1 = bf16[8,4,128,512]{3,2,1,0:T(8,128)(2,1)} async-done(((bf16[8,4,128,512]{3,2,1,0:T(8,128)(2,1)}), bf16[8,4,128,512]{3,2,1,0:T(8,128)(2,1)}, u32[]{:S(2)}, u32[]{:S(2)}) %all-to-all-start.1) | async-done | bytes 4194336 | tf_op jit(solution)/shard_map/all_to_all | solution.py:136
  233.9 7.6 copy.150
  241.4 7.3 reshape_reshape.7
  248.7 4.9 copy.153
  253.6 46.8 %while.88 = (s32[]{:T(128)}, f32[8,4,256,64]{2,3,1,0:T(8,128)}, f32[8,4,256]{2,1,0:T(4,128)S(1)}, bf16[8,4,256,64]{2,3,1,0:T(8,128)(2,1)S(1)}, bf16[8,4,1024,64]...) while((s32[]{:T(128)}, f32[8,4,256,64]{2,3,1,0:T(8,128)}, ...), condition=%wide.region_13.14_spmd.clone.clone, body=%wide.region_10.13_spmd.clone.sunk.clone | while | flops 277875712 | bytes 14076001 | solution.py:180
  308.0 5.2 reshape.568
  317.3 23.2 %fusion.182 = (f32[1024]{0:T(1024)S(1)}, f32[1024,2048]{1,0:T(8,128)S(1)}, f32[1024,2048]{1,0:T(8,128)}, f32[1024,2048]{1,0:T(8,128)}) fusion(f32[2048]{0:T(1024)S(1)} %copy-done.107, bf16[512,2048]{1,0:T(8,128)(2,1)S(1)} %copy-done, f32[1024,512]{1,0:T(8,128)S(1)} %get-tuple-element.785, f32[512]{0:T(512)S(1)} %copy-done.100, f32[512]{0:T(512)S(1)} %copy-done.91, ...), kind=kOutput, calls=%fused_computation.288 | convolution fusion | flops 2288516096 | bytes 29384704 | tf_op jit(solution)/shard_map/dot_general | solution.py:20
  349.5 13.5 %fusion.176 = (f32[2048]{0:T(1024)}, bf16[1024,2048]{1,0:T(8,128)(2,1)S(1)}, bf16[1024,2048]{1,0:T(8,128)(2,1)}) fusion(f32[1024,2048]{1,0:T(8,128)} %get-tuple-element.756, f32[1024]{0:T(1024)} %negate_multiply_fusion.5, f32[1024]{0:T(1024)S(1)} %get-tuple-element.776, f32[1024,2048]{1,0:T(8,128)S(1)} %get-tuple-element.755, ...), kind=kLoop, calls=%fused_computation.282 | loop fusion | flops 56621056 | bytes 41992192 | tf_op jit(solution)/shard_map/reduce_sum | solution.py:203
  363.0 6.6 multiply_reduce_fusion.5
  379.8 89.8 %while.89 = (s32[]{:T(128)}, bf16[8,4,256,64]{2,3,1,0:T(8,128)(2,1)S(1)}, bf16[8,4,1024,64]{2,3,0,1:T(8,128)(2,1)}, bf16[8,4,1024,64]{2,3,0,1:T(8,128)(2,1)}, bf...) while((s32[]{:T(128)}, ...), condition=%wide.region_28.29_spmd.clone.clone, body=%wide.region_26.28_spmd.clone.sunk.clone | while | flops 683674624 | bytes 36225148 | solution.py:219
  469.6 8.2 copy.172
  477.8 8.1 all-to-all-start.2
  504.9 7.8 copy.176
  517.5 57.6 %all-to-all-done.2 = bf16[1,4,1024,512]{3,1,0,2:T(4,128)(2,1)} async-done(((bf16[1,4,1024,512]{3,1,0,2:T(4,128)(2,1)}), bf16[1,4,1024,512]{3,1,0,2:T(4,128)(2,1)}, u32[]{:S(2)}, u32[]{:S(2)}) %all-to-all-start.2) | async-done | bytes 4194336 | tf_op jit(solution)/shard_map/all_to_all | solution.py:229
  575.1 7.8 all-to-all-start.3
  583.0 138.2 %while.90 = (s32[]{:T(128)}, bf16[8,4,256,64]{2,3,1,0:T(8,128)(2,1)}, bf16[8,4,256,64]{2,3,1,0:T(8,128)(2,1)}, bf16[8,4,256,64]{2,3,1,0:T(8,128)(2,1)}, f32[8,25...) while((s32[]{:T(128)}, ...), condition=%wide.region_34.35_spmd.clone.clone, body=%wide.region_31.34_spmd.clone.sunk.clone | while | flops 170851328 | bytes 12018829 | solution.py:269
  588.8 6.9 dynamic_update_slice.99
  606.0 6.9 dynamic_update_slice.99
  623.2 6.9 dynamic_update_slice.99
  640.4 6.9 dynamic_update_slice.99
  657.7 6.9 dynamic_update_slice.99
  674.9 6.9 dynamic_update_slice.99
  692.1 6.9 dynamic_update_slice.99
  709.3 6.9 dynamic_update_slice.99
  744.3 4.9 fusion.142
  749.1 5.5 fusion.146
  754.7 6.8 fusion.149
  781.5 49.2 %while.91 = (s32[]{:T(128)}, f32[511,8]{0,1:T(8,128)S(1)}, s32[4,64,256]{2,1,0:T(8,128)}, f32[4,8,64,256]{3,1,2,0:T(8,128)}) while((s32[]{:T(128)}, f32[511,8]{0,1:T(8,128)S(1)}, s32[4,64,256]{2,1,0:T(8,128)}, f32[4,8,64,256]{3,1,2,0:T(8,128)}) %tuple.234), condition=%wide.region_49.50_spmd.clone.clone, body=%wide.region_48.49_spmd.clone.sunk.clone | while | flops 812113920 | bytes 754179 | solution.py:284
  782.6 11.3 fusion.341
  794.7 11.3 fusion.341
  806.9 11.4 fusion.341
  819.2 11.3 fusion.341
  836.1 6.8 add_convert_fusion
  842.9 211.1 %all-reduce.7.cloned.1.call-done = (f32[512,512]{1,0:T(8,128)}, f32[512,512]{1,0:T(8,128)}, f32[512,512]{1,0:T(8,128)}, f32[512,512]{1,0:T(8,128)}, f32[512,512]...) async-done(((f32[512,512]{1,0:T(8,128)}, f32[512,512]{1,0:T(8,128)}, ...) | async-done | bytes 16777232 | tf_op jit(solution)/shard_map/psum | solution.py:304
  1057.9 158.2 %all-reduce.5.cloned.1.call-done = (f32[512]{0:T(512)}, f32[512]{0:T(512)}, f32[512]{0:T(512)}, f32[512]{0:T(512)}, f32[511,8]{0,1:T(8,128)}, /*index=5*/f32[8]{...) async-done(((f32[512]{0:T(512)}, f32[512]{0:T(512)}, ...) | async-done | bytes 71696 | tf_op jit(solution)/shard_map/psum | solution.py:304
  (688 shorter events, 446.0 us)
Async XLA Ops:
  7.2 309.7 %copy-start = (bf16[512,2048]{1,0:T(8,128)(2,1)S(1)}, bf16[512,2048]{1,0:T(8,128)(2,1)}, u32[]{:S(2)}) copy-start(bf16[512,2048]{1,0:T(8,128)(2,1)} %param.80) | copy-start | bytes 6291460
  14.0 6.4 copy-start.2
  14.0 124.3 %all-to-all-start = ((bf16[8,4,128,512]{3,2,1,0:T(8,128)(2,1)}), bf16[8,4,128,512]{3,2,1,0:T(8,128)(2,1)}, u32[]{:S(2)}, u32[]{:S(2)}) async-start(bf16[8,4,128,512]{3,2,1,0:T(8,128)(2,1)} %convolution_convert_fusion), calls=%async_computation | async-start | bytes 8388608 | tf_op jit(solution)/shard_map/all_to_all | solution.py:135
  37.5 5.2 copy-start.133
  46.6 5.0 copy-start.131
  138.3 95.5 %all-to-all-start.1 = ((bf16[8,4,128,512]{3,2,1,0:T(8,128)(2,1)}), bf16[8,4,128,512]{3,2,1,0:T(8,128)(2,1)}, u32[]{:S(2)}, u32[]{:S(2)}) async-start(bf16[8,4,128,512]{3,2,1,0:T(8,128)(2,1)} %add_convert_fusion.2), calls=%async_computation.1 | async-start | bytes 8388608 | tf_op jit(solution)/shard_map/all_to_all | solution.py:136
  144.6 37.3 %copy-start.123 = (f32[8]{0:T(128)S(1)}, f32[8]{0:T(128)}, u32[]{:S(2)}) copy-start(f32[8]{0:T(128)} %param.64) | copy-start | bytes 100
  248.7 4.9 copy-start.78
  308.0 5.2 copy-start.96
  308.0 5.2 copy-start.137
  308.0 5.2 copy-start.138
  316.4 24.0 %copy-start.9 = (f32[1024,512]{1,0:T(8,128)}, f32[1024,512]{1,0:T(8,128)S(1)}, u32[]{:S(2)}) copy-start(f32[1024,512]{1,0:T(8,128)S(1)} %get-tuple-element.785) | copy-start | bytes 6291460
  317.3 23.2 %copy-start.41 = (bf16[1024,512]{1,0:T(8,128)(2,1)S(1)}, bf16[1024,512]{1,0:T(8,128)(2,1)}, u32[]{:S(2)}) copy-start(bf16[1024,512]{1,0:T(8,128)(2,1)} %bitcast_convert_fusion) | copy-start | bytes 3145732
  317.3 23.2 %copy-start.90 = (f32[2048]{0:T(1024)S(1)}, f32[2048]{0:T(1024)}, u32[]{:S(2)}) copy-start(f32[2048]{0:T(1024)} %param.82) | copy-start | bytes 24580
  317.3 23.2 %copy-start.127 = (bf16[2048,512]{1,0:T(8,128)(2,1)S(1)}, bf16[2048,512]{1,0:T(8,128)(2,1)}, u32[]{:S(2)}) copy-start(bf16[2048,512]{1,0:T(8,128)(2,1)} %param.84) | copy-start | bytes 6291460
  363.0 6.6 copy-start.7
  363.0 6.6 copy-start.10
  363.0 6.6 copy-start.92
  469.6 22.5 %copy-start.23 = (bf16[8,4,256,64]{2,3,1,0:T(8,128)(2,1)}, bf16[8,4,256,64]{2,3,1,0:T(8,128)(2,1)S(1)}, u32[]{:S(2)}) copy-start(bf16[8,4,256,64]{2,3,1,0:T(8,128)(2,1)S(1)} %get-tuple-element.291) | copy-start | bytes 3145732
  477.8 97.3 %all-to-all-start.2 = ((bf16[1,4,1024,512]{3,1,0,2:T(4,128)(2,1)}), bf16[1,4,1024,512]{3,1,0,2:T(4,128)(2,1)}, u32[]{:S(2)}, u32[]{:S(2)}) async-start(bf16[1,4,1024,512]{3,1,0,2:T(4,128)(2,1)} %copy.172), calls=%async_computation.2 | async-start | bytes 8388608 | tf_op jit(solution)/shard_map/all_to_all | solution.py:229
  485.8 4.8 copy-start.3
  485.9 4.7 copy-start.80
  485.9 4.7 copy-start.82
  485.9 4.7 copy-start.93
  485.9 4.7 copy-start.106
  504.9 7.8 copy-start.124
  517.5 65.5 %copy-start.27 = (pred[256,256]{0,1:T(8,128)(4,1)S(1)}, pred[256,256]{0,1:T(8,128)(4,1)}, u32[]{:S(2)}) copy-start(pred[256,256]{0,1:T(8,128)(4,1)} %copy-done.26) | copy-start | bytes 196612
  517.5 65.5 %copy-start.70 = (pred[4,256]{1,0:T(4,128)(4,1)S(1)}, pred[4,256]{1,0:T(4,128)(4,1)}, u32[]{:S(2)}) copy-start(pred[4,256]{1,0:T(4,128)(4,1)} %copy-done.69) | copy-start | bytes 3076
  575.1 179.6 %all-to-all-start.3 = ((bf16[1,4,1024,512]{3,1,0,2:T(4,128)(2,1)}), bf16[1,4,1024,512]{3,1,0,2:T(4,128)(2,1)}, u32[]{:S(2)}, u32[]{:S(2)}) async-start(bf16[1,4,1024,512]{3,1,0,2:T(4,128)(2,1)} %copy.176), calls=%async_computation.3 | async-start | bytes 8388608 | tf_op jit(solution)/shard_map/all_to_all | solution.py:236
  582.9 471.0 %all-reduce.7.cloned.1.call-start = ((), (), s32[]{:S(2)}) async-start(), calls=%async_computation.5 | async-start | bytes 33554432 | tf_op jit(solution)/shard_map/psum | solution.py:304
  723.8 4.9 copy-start.28
  725.0 5.4 copy-start.32
  726.9 5.2 copy-start.30
  730.4 5.7 copy-start.139
  744.3 4.9 copy-start.126
  761.5 454.7 %all-reduce.5.cloned.1.call-start = ((), (), s32[]{:S(2)}) async-start(), calls=%async_computation.4 | async-start | bytes 144384 | tf_op jit(solution)/shard_map/psum | solution.py:304
  771.0 5.6 copy-start.128
  781.5 49.9 %copy-start.67 = (bf16[512,512]{1,0:T(8,128)(2,1)S(1)}, bf16[512,512]{1,0:T(8,128)(2,1)}, u32[]{:S(2)}) copy-start(bf16[512,512]{1,0:T(8,128)(2,1)} %param.72) | copy-start | bytes 1572868
  1053.9 164.7 %copy-start.51 = (f32[512,512]{1,0:T(8,128)S(1)}, f32[512,512]{1,0:T(8,128)}, u32[]{:S(2)}) copy-start(f32[512,512]{1,0:T(8,128)} %get-tuple-element.1367) | copy-start | bytes 3145732
  1056.6 163.5 %copy-start.50 = (f32[512,512]{1,0:T(8,128)S(1)}, f32[512,512]{1,0:T(8,128)}, u32[]{:S(2)}) copy-start(f32[512,512]{1,0:T(8,128)} %get-tuple-element.1369) | copy-start | bytes 3145732
  1221.2 4.9 copy-start.118
  1221.2 5.4 copy-start.47
  1223.9 4.9 copy-start.115
  1223.9 5.5 copy-start.114
  1223.9 6.1 copy-start.46
  1226.6 4.9 copy-start.112
  1226.6 5.5 copy-start.111
  1226.6 6.0 copy-start.35
  (100 other events, 230.6 us)
Sparse Core Ops, SparseCore 0:
  761.6 292.2 all-reduce.6
  1063.2 152.8 all-reduce.4
where the time goes:
time: 1260 us; the launch traced here: 1250 us
  waiting for transfers between devices  440 us (35%)
  matrix products  425 us (34%)
  local copies, waits for them, and re-layouts  266 us (21%)
  other arithmetic  70.4 us (6%)
  starting transfers between devices  28.6 us (2%)
  between operations  15.7 us (1%)
    psum x2, waiting for transfers between devices, local(): lax.psum((sum_self_gain, sum_self_shift, sum_query_weight, sum_query_bias...  369 us
    unnamed x333, local copies, waits for them, and re-layouts  73.7 us
    dot_general x4, matrix products, bias_rows(): jnp.einsum('qkb,bh->hqk', one_hot, position_table, precision=lax.Precisio...  73.6 us
    all_to_all x1, waiting for transfers between devices, local(): lax.all_to_all(low_key_two.reshape(1, seq_count, mem_total, model_width),...  57.6 us
    dynamic_update_slice x16, local copies, waits for them, and re-layouts, local(): lax.map(self_backward, (heads_query, heads_key, heads_value, bias_heads,...  56.4 us
    dot_general x32, matrix products, scores_of(): jnp.einsum('sqd,skd->sqk', query_block, key_block, preferred_element_type...  53.1 us
    dot_general x10, matrix products, matmul(): return jnp.dot(left_side, right_side, preferred_element_type=jnp.float32)  50.8 us
    dot_general x4, matrix products, bucket_sums(): jnp.einsum('qkb,hqk->bh', one_hot, packed[1], precision=lax.Precision.HIG...  45.4 us
  transfers between devices with their start and end apart: 6, of which 4 were waited for; matrix products, arithmetic and copies ran while one was open for 37% of the time, Pallas kernels for 0%

commit v1 on v0

--- a/solution.py
+++ b/solution.py
@@ -301,41 +301,40 @@
     tokens_gradient = (
         (grad_one + part_zero).astype(jnp.bfloat16).reshape(seq_count, length, model_width)
     )
-    totals = lax.psum(
-        (
-            sum_self_gain,
-            sum_self_shift,
-            sum_query_weight,
-            sum_query_bias,
-            sum_key_weight,
-            sum_value_weight,
-            sum_value_bias,
-            sum_position_table,
-            sum_head_scale,
-            sum_output_weight,
-            sum_output_bias,
-            sum_cross_gain,
-            sum_cross_shift,
-            sum_cross_query,
-            sum_cross_query_bias,
-            sum_cross_key,
-            sum_cross_value,
-            sum_cross_value_bias,
-            sum_post_gain,
-            sum_post_shift,
-            sum_cross_output,
-            sum_cross_output_bias,
-            sum_feed_gain,
-            sum_feed_shift,
-            sum_inner_weight,
-            sum_inner_bias,
-            sum_inner_gain,
-            sum_inner_shift,
-            sum_outer_weight,
-            sum_outer_bias,
-        ),
-        ("dp", "rep"),
-    )
+    totals = (
+        sum_self_gain,
+        sum_self_shift,
+        sum_query_weight,
+        sum_query_bias,
+        sum_key_weight,
+        sum_value_weight,
+        sum_value_bias,
+        sum_position_table,
+        sum_head_scale,
+        sum_output_weight,
+        sum_output_bias,
+        sum_cross_gain,
+        sum_cross_shift,
+        sum_cross_query,
+        sum_cross_query_bias,
+        sum_cross_key,
+        sum_cross_value,
+        sum_cross_value_bias,
+        sum_post_gain,
+        sum_post_shift,
+        sum_cross_output,
+        sum_cross_output_bias,
+        sum_feed_gain,
+        sum_feed_shift,
+        sum_inner_weight,
+        sum_inner_bias,
+        sum_inner_gain,
+        sum_inner_shift,
+        sum_outer_weight,
+        sum_outer_bias,
+    )
+    for mesh_axis in ("rep", "dp"):
+        totals = lax.psum(totals, mesh_axis)
     return (layer_output, tokens_gradient, memory_gradient) + tuple(totals)
 
 

time: 1260 us -> 1750 us (1.39)
  waiting for transfers between devices: 440 us -> 926 us
    psum x2 -> x4, waiting for transfers between devices: 369 us -> 855 us  [local(): totals = lax.psum(totals, mesh_axis)]
    unnamed x333 -> x331, local copies, waits for them, and re-layouts: 73.7 us -> 73.9 us
  transfers between devices with their start and end apart: 6 -> 8, of which waited for: 4 -> 6; matrix products, arithmetic and copies ran while one was open for 37% -> 27% of each run, Pallas kernels for 0% -> 0%
where the time goes in v1:
time: 1750 us; the launch traced here: 1740 us
  waiting for transfers between devices  926 us (53%)
  matrix products  426 us (24%)
  local copies, waits for them, and re-layouts  265 us (15%)
  other arithmetic  73.5 us (4%)
  starting transfers between devices  28.6 us (2%)
    psum x4, waiting for transfers between devices, local(): totals = lax.psum(totals, mesh_axis)  855 us
    unnamed x331, local copies, waits for them, and re-layouts  73.9 us
    dot_general x4, matrix products, bias_rows(): jnp.einsum('qkb,bh->hqk', one_hot, position_table, precision=lax.Precisio...  73.6 us
    all_to_all x1, waiting for transfers between devices, local(): lax.all_to_all(low_key_two.reshape(1, seq_count, mem_total, model_width),...  57.8 us
    dynamic_update_slice x16, local copies, waits for them, and re-layouts, local(): lax.map(self_backward, (heads_query, heads_key, heads_value, bias_heads,...  56.3 us
    dot_general x32, matrix products, scores_of(): jnp.einsum('sqd,skd->sqk', query_block, key_block, preferred_element_type...  53.1 us
    dot_general x10, matrix products, matmul(): return jnp.dot(left_side, right_side, preferred_element_type=jnp.float32)  52.4 us
    dot_general x4, matrix products, bucket_sums(): jnp.einsum('qkb,hqk->bh', one_hot, packed[1], precision=lax.Precision.HIG...  45.3 us
  transfers between devices with their start and end apart: 8, of which 6 were waited for; matrix products, arithmetic and copies ran while one was open for 27% of the time, Pallas kernels for 0%

profile of v1, /device:TPU:10, one launch (start us, length us, event | category | flops | bytes accessed | tf_op | source)
XLA Modules:
  0.0 1735.6 jit_solution(18234448428807387149)
XLA Ops:
  7.2 6.8 convolution_convert_fusion
  14.0 6.3 all-to-all-start
  51.6 77.0 %while.86 = (s32[]{:T(128)}, f32[4,8,64,256]{3,1,2,0:T(8,128)}, s32[4,64,256]{2,1,0:T(8,128)}, f32[511,8]{0,1:T(8,128)S(1)}) while((s32[]{:T(128)}, f32[4,8,64,256]{3,1,2,0:T(8,128)}, s32[4,64,256]{2,1,0:T(8,128)}, f32[511,8]{0,1:T(8,128)S(1)}) %tuple.241), condition=%wide.region_3.4_spmd.clone.clone, body=%wide.region_2.3_spmd.clone.sunk.clone | while | flops 812105728 | bytes 737817 | solution.py:155
  52.5 18.4 %fusion.310 = f32[4,8,64,256]{3,1,2,0:T(8,128)} fusion(f32[4,8,64,256]{3,1,2,0:T(8,128)} %get-tuple-element.1256, s32[]{:T(128)} %get-tuple-element.1255, s32[64,256]{1,0:T(8,128)S(1)} %dynamic-slice_bitcast_fusion.18, f32[511,8]{0,1:T(8,128)S(1)} %get-tuple-element.1262), kind=kOutput, calls=%fused_computation.10.clone.1.clone | convolution fusion | flops 812105728 | bytes 606688 | tf_op jit(solution)/shard_map/while/body/eval_jaxpr/qkb,bh->hqk/dot_general | solution.py:153
  71.7 18.4 %fusion.310 = f32[4,8,64,256]{3,1,2,0:T(8,128)} fusion(f32[4,8,64,256]{3,1,2,0:T(8,128)} %get-tuple-element.1256, s32[]{:T(128)} %get-tuple-element.1255, s32[64,256]{1,0:T(8,128)S(1)} %dynamic-slice_bitcast_fusion.18, f32[511,8]{0,1:T(8,128)S(1)} %get-tuple-element.1262), kind=kOutput, calls=%fused_computation.10.clone.1.clone | convolution fusion | flops 812105728 | bytes 606688 | tf_op jit(solution)/shard_map/while/body/eval_jaxpr/qkb,bh->hqk/dot_general | solution.py:153
  91.0 18.4 %fusion.310 = f32[4,8,64,256]{3,1,2,0:T(8,128)} fusion(f32[4,8,64,256]{3,1,2,0:T(8,128)} %get-tuple-element.1256, s32[]{:T(128)} %get-tuple-element.1255, s32[64,256]{1,0:T(8,128)S(1)} %dynamic-slice_bitcast_fusion.18, f32[511,8]{0,1:T(8,128)S(1)} %get-tuple-element.1262), kind=kOutput, calls=%fused_computation.10.clone.1.clone | convolution fusion | flops 812105728 | bytes 606688 | tf_op jit(solution)/shard_map/while/body/eval_jaxpr/qkb,bh->hqk/dot_general | solution.py:153
  110.2 18.4 %fusion.310 = f32[4,8,64,256]{3,1,2,0:T(8,128)} fusion(f32[4,8,64,256]{3,1,2,0:T(8,128)} %get-tuple-element.1256, s32[]{:T(128)} %get-tuple-element.1255, s32[64,256]{1,0:T(8,128)S(1)} %dynamic-slice_bitcast_fusion.18, f32[511,8]{0,1:T(8,128)S(1)} %get-tuple-element.1262), kind=kOutput, calls=%fused_computation.10.clone.1.clone | convolution fusion | flops 812105728 | bytes 606688 | tf_op jit(solution)/shard_map/while/body/eval_jaxpr/qkb,bh->hqk/dot_general | solution.py:153
  131.6 6.7 add_convert_fusion.2
  138.3 6.3 all-to-all-start.1
  144.6 37.2 %while.87 = (s32[]{:T(128)}, f32[8,4,256,64]{2,1,3,0:T(4,128)}, f32[8,4,256]{2,1,0:T(4,128)S(1)}, bf16[8,4,256,64]{2,3,1,0:T(8,128)(2,1)}, bf16[8,4,256,64]{2,3,...) while((s32[]{:T(128)}, f32[8,4,256,64]{2,1,3,0:T(4,128)}, ...), condition=%wide.region_7.8_spmd.clone.clone, body=%wide.region_4.7_spmd.clone.sunk.clone | while | flops 69467136 | bytes 5213285 | solution.py:165
  201.1 7.6 copy.149
  208.7 7.3 reshape_reshape.6
  220.8 13.0 all-to-all-done.1
  233.8 7.6 copy.150
  241.4 7.3 reshape_reshape.7
  253.6 46.8 %while.88 = (s32[]{:T(128)}, f32[8,4,256,64]{2,3,1,0:T(8,128)}, f32[8,4,256]{2,1,0:T(4,128)S(1)}, bf16[8,4,256,64]{2,3,1,0:T(8,128)(2,1)S(1)}, bf16[8,4,1024,64]...) while((s32[]{:T(128)}, f32[8,4,256,64]{2,3,1,0:T(8,128)}, ...), condition=%wide.region_13.14_spmd.clone.clone, body=%wide.region_10.13_spmd.clone.sunk.clone | while | flops 277875712 | bytes 14076001 | solution.py:180
  307.9 5.2 reshape.568
  317.2 23.2 %fusion.182 = (f32[1024]{0:T(1024)S(1)}, f32[1024,2048]{1,0:T(8,128)S(1)}, f32[1024,2048]{1,0:T(8,128)}, f32[1024,2048]{1,0:T(8,128)}) fusion(f32[2048]{0:T(1024)S(1)} %copy-done.107, bf16[512,2048]{1,0:T(8,128)(2,1)S(1)} %copy-done, f32[1024,512]{1,0:T(8,128)S(1)} %get-tuple-element.815, f32[512]{0:T(512)S(1)} %copy-done.100, f32[512]{0:T(512)S(1)} %copy-done.91, ...), kind=kOutput, calls=%fused_computation.288 | convolution fusion | flops 2288516096 | bytes 29384704 | tf_op jit(solution)/shard_map/dot_general | solution.py:20
  349.4 13.5 fusion.176
  363.0 6.6 multiply_reduce_fusion.5
  379.9 89.5 %while.89 = (s32[]{:T(128)}, bf16[8,4,256,64]{2,3,1,0:T(8,128)(2,1)S(1)}, bf16[8,4,1024,64]{2,3,0,1:T(8,128)(2,1)}, bf16[8,4,1024,64]{2,3,0,1:T(8,128)(2,1)}, bf...) while((s32[]{:T(128)}, ...), condition=%wide.region_28.29_spmd.clone.clone, body=%wide.region_26.28_spmd.clone.sunk.clone | while | flops 683674624 | bytes 36225148 | solution.py:219
  469.4 8.2 copy.172
  477.6 8.1 all-to-all-start.2
  504.7 7.8 copy.176
  517.1 57.8 %all-to-all-done.2 = bf16[1,4,1024,512]{3,1,0,2:T(4,128)(2,1)} async-done(((bf16[1,4,1024,512]{3,1,0,2:T(4,128)(2,1)}), bf16[1,4,1024,512]{3,1,0,2:T(4,128)(2,1)}, u32[]{:S(2)}, u32[]{:S(2)}) %all-to-all-start.2) | async-done | bytes 4194336 | tf_op jit(solution)/shard_map/all_to_all | solution.py:229
  574.9 7.8 all-to-all-start.3
  582.7 138.1 %while.90 = (s32[]{:T(128)}, bf16[8,4,256,64]{2,3,1,0:T(8,128)(2,1)}, bf16[8,4,256,64]{2,3,1,0:T(8,128)(2,1)}, bf16[8,4,256,64]{2,3,1,0:T(8,128)(2,1)}, f32[8,25...) while((s32[]{:T(128)}, ...), condition=%wide.region_34.35_spmd.clone.clone, body=%wide.region_31.34_spmd.clone.sunk.clone | while | flops 170851328 | bytes 12018829 | solution.py:269
  588.5 6.9 dynamic_update_slice.99
  605.7 6.9 dynamic_update_slice.99
  622.9 6.9 dynamic_update_slice.99
  640.1 6.9 dynamic_update_slice.99
  657.3 6.9 dynamic_update_slice.99
  674.5 6.9 dynamic_update_slice.99
  691.8 6.9 dynamic_update_slice.99
  709.0 6.9 dynamic_update_slice.99
  748.7 5.5 fusion.146
  754.3 6.8 fusion.149
  775.8 48.7 %while.91 = (s32[]{:T(128)}, f32[511,8]{0,1:T(8,128)S(1)}, s32[4,64,256]{2,1,0:T(8,128)}, f32[4,8,64,256]{3,1,2,0:T(8,128)}) while((s32[]{:T(128)}, f32[511,8]{0,1:T(8,128)S(1)}, s32[4,64,256]{2,1,0:T(8,128)}, f32[4,8,64,256]{3,1,2,0:T(8,128)}) %tuple.240), condition=%wide.region_56.57_spmd.clone.clone, body=%wide.region_55.56_spmd.clone.sunk.clone | while | flops 812113920 | bytes 754179 | solution.py:284
  776.7 11.3 fusion.341
  788.8 11.3 fusion.341
  801.0 11.3 fusion.341
  813.2 11.3 fusion.341
  825.2 230.1 %all-reduce.15.cloned.1.call-done = (f32[512,512]{1,0:T(8,128)}, f32[512,512]{1,0:T(8,128)}, f32[512,512]{1,0:T(8,128)}, f32[512,512]{1,0:T(8,128)}, f32[512,512...) async-done(((f32[512,512]{1,0:T(8,128)}, f32[512,512]{1,0:T(8,128)}, ...) | async-done | bytes 16777232 | tf_op jit(solution)/shard_map/psum | solution.py:337
  1059.8 5.0 add_convert_fusion.5
  1064.8 30.1 %all-reduce.13.cloned.1.call-done = (f32[512]{0:T(512)}, f32[512]{0:T(512)}, f32[512]{0:T(512)}, f32[512]{0:T(512)}, f32[511,8]{0,1:T(8,128)}, /*index=5*/f32[8]...) async-done(((f32[512]{0:T(512)}, f32[512]{0:T(512)}, ...) | async-done | bytes 71696 | tf_op jit(solution)/shard_map/psum | solution.py:337
  1099.6 6.7 add_convert_fusion
  1106.3 514.2 %all-reduce.11.cloned.1.call-done = (f32[512,512]{1,0:T(8,128)}, f32[512,512]{1,0:T(8,128)}, f32[512,512]{1,0:T(8,128)}, f32[512,512]{1,0:T(8,128)}, f32[512,512...) async-done(((f32[512,512]{1,0:T(8,128)}, f32[512,512]{1,0:T(8,128)}, ...) | async-done | bytes 16777232 | tf_op jit(solution)/shard_map/psum | solution.py:337
  1624.5 80.5 %all-reduce.9.cloned.1.call-done = (f32[512]{0:T(512)}, f32[512]{0:T(512)}, f32[512]{0:T(512)}, f32[512]{0:T(512)}, f32[511,8]{0,1:T(8,128)}, /*index=5*/f32[8]{...) async-done(((f32[512]{0:T(512)}, f32[512]{0:T(512)}, ...) | async-done | bytes 71696 | tf_op jit(solution)/shard_map/psum | solution.py:337
  (692 shorter events, 459.5 us)
Async XLA Ops:
  7.2 309.7 %copy-start = (bf16[512,2048]{1,0:T(8,128)(2,1)S(1)}, bf16[512,2048]{1,0:T(8,128)(2,1)}, u32[]{:S(2)}) copy-start(bf16[512,2048]{1,0:T(8,128)(2,1)} %param.80) | copy-start | bytes 6291460
  14.0 6.4 copy-start.2
  14.0 124.2 %all-to-all-start = ((bf16[8,4,128,512]{3,2,1,0:T(8,128)(2,1)}), bf16[8,4,128,512]{3,2,1,0:T(8,128)(2,1)}, u32[]{:S(2)}, u32[]{:S(2)}) async-start(bf16[8,4,128,512]{3,2,1,0:T(8,128)(2,1)} %convolution_convert_fusion), calls=%async_computation | async-start | bytes 8388608 | tf_op jit(solution)/shard_map/all_to_all | solution.py:135
  37.5 5.2 copy-start.132
  46.6 5.0 copy-start.130
  138.3 95.6 %all-to-all-start.1 = ((bf16[8,4,128,512]{3,2,1,0:T(8,128)(2,1)}), bf16[8,4,128,512]{3,2,1,0:T(8,128)(2,1)}, u32[]{:S(2)}, u32[]{:S(2)}) async-start(bf16[8,4,128,512]{3,2,1,0:T(8,128)(2,1)} %add_convert_fusion.2), calls=%async_computation.1 | async-start | bytes 8388608 | tf_op jit(solution)/shard_map/all_to_all | solution.py:136
  144.6 37.3 %copy-start.123 = (f32[8]{0:T(128)S(1)}, f32[8]{0:T(128)}, u32[]{:S(2)}) copy-start(f32[8]{0:T(128)} %param.64) | copy-start | bytes 100
  248.7 4.9 copy-start.78
  307.9 5.2 copy-start.96
  307.9 5.2 copy-start.136
  307.9 5.2 copy-start.137
  316.4 24.0 %copy-start.8 = (f32[1024,512]{1,0:T(8,128)}, f32[1024,512]{1,0:T(8,128)S(1)}, u32[]{:S(2)}) copy-start(f32[1024,512]{1,0:T(8,128)S(1)} %get-tuple-element.815) | copy-start | bytes 6291460
  317.2 23.2 %copy-start.41 = (bf16[1024,512]{1,0:T(8,128)(2,1)S(1)}, bf16[1024,512]{1,0:T(8,128)(2,1)}, u32[]{:S(2)}) copy-start(bf16[1024,512]{1,0:T(8,128)(2,1)} %bitcast_convert_fusion) | copy-start | bytes 3145732
  317.2 23.2 %copy-start.90 = (f32[2048]{0:T(1024)S(1)}, f32[2048]{0:T(1024)}, u32[]{:S(2)}) copy-start(f32[2048]{0:T(1024)} %param.82) | copy-start | bytes 24580
  317.2 23.2 %copy-start.127 = (bf16[2048,512]{1,0:T(8,128)(2,1)S(1)}, bf16[2048,512]{1,0:T(8,128)(2,1)}, u32[]{:S(2)}) copy-start(bf16[2048,512]{1,0:T(8,128)(2,1)} %param.84) | copy-start | bytes 6291460
  363.0 6.6 copy-start.6
  363.0 6.6 copy-start.9
  363.0 6.6 copy-start.92
  469.3 22.5 %copy-start.23 = (bf16[8,4,256,64]{2,3,1,0:T(8,128)(2,1)}, bf16[8,4,256,64]{2,3,1,0:T(8,128)(2,1)S(1)}, u32[]{:S(2)}) copy-start(bf16[8,4,256,64]{2,3,1,0:T(8,128)(2,1)S(1)} %get-tuple-element.291) | copy-start | bytes 3145732
  477.6 97.3 %all-to-all-start.2 = ((bf16[1,4,1024,512]{3,1,0,2:T(4,128)(2,1)}), bf16[1,4,1024,512]{3,1,0,2:T(4,128)(2,1)}, u32[]{:S(2)}, u32[]{:S(2)}) async-start(bf16[1,4,1024,512]{3,1,0,2:T(4,128)(2,1)} %copy.172), calls=%async_computation.2 | async-start | bytes 8388608 | tf_op jit(solution)/shard_map/all_to_all | solution.py:229
  485.6 4.8 copy-start.3
  485.6 4.7 copy-start.80
  485.7 4.7 copy-start.82
  485.7 4.7 copy-start.93
  504.7 7.8 copy-start.124
  517.1 65.6 %copy-start.27 = (pred[256,256]{0,1:T(8,128)(4,1)S(1)}, pred[256,256]{0,1:T(8,128)(4,1)}, u32[]{:S(2)}) copy-start(pred[256,256]{0,1:T(8,128)(4,1)} %copy-done.26) | copy-start | bytes 196612
  517.1 65.6 %copy-start.70 = (pred[4,256]{1,0:T(4,128)(4,1)S(1)}, pred[4,256]{1,0:T(4,128)(4,1)}, u32[]{:S(2)}) copy-start(pred[4,256]{1,0:T(4,128)(4,1)} %copy-done.69) | copy-start | bytes 3076
  574.9 179.4 %all-to-all-start.3 = ((bf16[1,4,1024,512]{3,1,0,2:T(4,128)(2,1)}), bf16[1,4,1024,512]{3,1,0,2:T(4,128)(2,1)}, u32[]{:S(2)}, u32[]{:S(2)}) async-start(bf16[1,4,1024,512]{3,1,0,2:T(4,128)(2,1)} %copy.176), calls=%async_computation.3 | async-start | bytes 8388608 | tf_op jit(solution)/shard_map/all_to_all | solution.py:236
  582.7 472.6 %all-reduce.15.cloned.1.call-start = ((), (), s32[]{:S(2)}) async-start(), calls=%async_computation.7 | async-start | bytes 33554432 | tf_op jit(solution)/shard_map/psum | solution.py:337
  723.4 4.9 copy-start.28
  724.6 5.4 copy-start.32
  726.6 5.2 copy-start.30
  730.0 5.6 copy-start.138
  743.9 4.9 copy-start.126
  761.1 333.8 %all-reduce.13.cloned.1.call-start = ((), (), s32[]{:S(2)}) async-start(), calls=%async_computation.6 | async-start | bytes 144384 | tf_op jit(solution)/shard_map/psum | solution.py:337
  825.1 795.4 %all-reduce.11.cloned.1.call-start = ((), (), s32[]{:S(2)}) async-start(), calls=%async_computation.5 | async-start | bytes 33554432 | tf_op jit(solution)/shard_map/psum | solution.py:337
  1055.3 649.7 %all-reduce.9.cloned.1.call-start = ((), (), s32[]{:S(2)}) async-start(), calls=%async_computation.4 | async-start | bytes 144384 | tf_op jit(solution)/shard_map/psum | solution.py:337
  1059.8 35.1 %copy-start.67 = (bf16[512,512]{1,0:T(8,128)(2,1)S(1)}, bf16[512,512]{1,0:T(8,128)(2,1)}, u32[]{:S(2)}) copy-start(bf16[512,512]{1,0:T(8,128)(2,1)} %param.72) | copy-start | bytes 1572868
  1620.5 87.0 %copy-start.54 = (f32[512,512]{1,0:T(8,128)S(1)}, f32[512,512]{1,0:T(8,128)}, u32[]{:S(2)}) copy-start(f32[512,512]{1,0:T(8,128)} %get-tuple-element.1397) | copy-start | bytes 3145732
  1623.2 85.8 %copy-start.53 = (f32[512,512]{1,0:T(8,128)S(1)}, f32[512,512]{1,0:T(8,128)}, u32[]{:S(2)}) copy-start(f32[512,512]{1,0:T(8,128)} %get-tuple-element.1399) | copy-start | bytes 3145732
  1710.1 4.9 copy-start.118
  1710.1 5.4 copy-start.48
  1712.8 4.9 copy-start.115
  1712.8 5.5 copy-start.114
  1712.8 6.1 copy-start.46
  1715.5 4.9 copy-start.112
  1715.5 5.5 copy-start.111
  1715.5 6.0 copy-start.35
  (101 other events, 238.9 us)
Sparse Core Ops, SparseCore 0:
  761.2 294.0 all-reduce.14
  1062.0 32.8 all-reduce.12
  1102.5 517.9 all-reduce.10
  1627.4 77.5 all-reduce.8
